TPU v7x, 256 devices: a whole 4x4x8 slice. The times are simulated.
256 devices in a mesh: dp: 32 (over x_hi, z, core), tensor: 8 (over y, x_lo).
Axes of the slice: x: 4 (x_hi: 2, x_lo: 2; x = x_hi * 2 + x_lo), y: 4, z: 8, core: 2. Of those that a mesh axis runs over, the one named last changes fastest.
Arguments:
- tokens: bfloat16 [32768, 8192], P(('dp', 'tensor')), may hold values from -6 to 6
- out_grad: bfloat16 [32768, 26624], P('dp', 'tensor')
- delta: float32 [8, 128, 128, 128], P('tensor', 'dp'), may hold values from -3 to 3
- block_rows: int32 [1024], P('tensor'), may hold values from 0 to 63, as said below
- block_cols: int32 [1024], P('tensor'), may hold values from 0 to 25, as said below
- block_count: int32 [8], P('tensor'), may hold values from 1 to 128, as said below
Outputs:
- new_delta: float32 [8, 128, 128, 128], P('tensor', 'dp')
Inputs may be any that keep to these rules, and one draw needn't show every extreme that they name: `block_rows`: entry t * 128 + k names the row block of slot k of tensor shard t; the slots of one shard name distinct pairs of row and column block. `block_cols`: entry t * 128 + k names the column block, counted within shard t's columns, of slot k of shard t. Slots 0 to block_count[t] - 1 of shard t are live, the rest are padding; some shard has all 128 live.
All inputs are finite; a program needn't handle non-finite values.
Results may differ from a plain program's by a relative error of at most 0.0003.
Values may be sent and summed in bfloat16 or wider, within the bound.
No kernel may reach another device: no remote copies, remote signals or barrier semaphores. Data moves between devices by JAX's collectives and lax.ppermute only.
A program may use at most 192 MiB of HBM per device.

v0:
```python
import math
import jax
import jax.numpy as jnp
from jax import lax
from jax.sharding import PartitionSpec as P

GROUP = 32


def on_device(tokens, out_grad, delta, block_rows, block_cols, block_count):
    slot_count = block_rows.shape[0]
    block_size = delta.shape[-1]
    row_blocks = tokens.shape[1] // block_size
    col_blocks = out_grad.shape[1] // block_size
    group_trips = slot_count // GROUP
    zero_grads = jnp.zeros((slot_count, block_size, block_size), jnp.float32)
    shard_rows = lax.all_gather(tokens, "tensor", axis=0, tiled=True)
    row_count = shard_rows.shape[0]
    token_tiles = shard_rows.reshape(row_count, row_blocks, block_size)
    grad_tiles = out_grad.reshape(row_count, col_blocks, block_size)

    def one_group(group_index, partial_sum):
        row_ids = lax.dynamic_slice_in_dim(block_rows, group_index * GROUP, GROUP)
        col_ids = lax.dynamic_slice_in_dim(block_cols, group_index * GROUP, GROUP)
        token_cols = jnp.take(token_tiles, row_ids, axis=1)
        grad_cols = jnp.take(grad_tiles, col_ids, axis=1)
        partial_value = jnp.einsum(
            "rkc,rkd->kcd", token_cols, grad_cols, preferred_element_type=jnp.float32
        )
        previous = lax.dynamic_slice_in_dim(partial_sum, group_index * GROUP, GROUP, 0)
        return lax.dynamic_update_slice_in_dim(
            partial_sum, previous + partial_value, group_index * GROUP, 0
        )

    block_grads = lax.fori_loop(0, group_trips, one_group, zero_grads)
    live_mask = (jnp.arange(slot_count, dtype=jnp.int32) < block_count[0]).astype(jnp.float32)
    block_grads = block_grads * live_mask[:, None, None]
    cycle_size = lax.axis_size("tensor")
    norm_limit = block_size * math.sqrt(cycle_size * slot_count)
    share_len = delta.shape[1]
    summed = lax.psum(block_grads, "dp")
    square_sum = lax.psum(jnp.sum(summed * summed), "tensor")
    own_share = lax.dynamic_slice_in_dim(summed, lax.axis_index("dp") * share_len, share_len, 0)
    factor = jnp.minimum(jnp.float32(1.0), norm_limit / jnp.sqrt(square_sum + 1e-06))
    return delta - 0.5 * factor * own_share[None]


def solution(mesh):
    return jax.shard_map(
        on_device,
        mesh=mesh,
        in_specs=(
            P(("dp", "tensor"), None),
            P("dp", "tensor"),
            P("tensor", "dp", None, None),
            P("tensor"),
            P("tensor"),
            P("tensor"),
        ),
        out_specs=P("tensor", "dp", None, None),
        check_vma=False,
    )
```

profile of v0, /device:TPU:4, one launch (start us, length us, event | category | flops | bytes accessed | tf_op | source)
XLA Modules:
  0.0 820.9 jit_solution(13977758874296105967)
XLA Ops:
  6.5 4.1 copy.13
  10.7 10.0 %copy.14 = bf16[1024,3328]{0,1:T(8,128)(2,1)} copy(bf16[1024,3328]{1,0:T(8,128)(2,1)} %param.9) | data formatting | bytes 13631488 | tf_op args[1]
  20.7 10.0 %copy.16 = bf16[1024,26,128]{2,0,1:T(8,128)(2,1)} copy(bf16[1024,26,128]{0,2,1:T(8,128)(2,1)} %bitcast.20) | data formatting | bytes 13631488 | tf_op jit(solution)/shard_map/while | solution.py:35
  31.3 310.0 %all-gather.2.cloned.1.call-done = bf16[1024,8192]{0,1:T(8,128)(2,1)} async-done(((bf16[128,8192]{0,1:T(8,128)(2,1)}), bf16[1024,8192]{0,1:T(8,128)(2,1)}) %all-gather.2.cloned.1.call-update) | async-done | bytes 16777232 | tf_op jit(solution)/shard_map/all_gather | solution.py:17
  341.3 22.4 %copy.15 = bf16[1024,64,128]{2,0,1:T(8,128)(2,1)} copy(bf16[1024,64,128]{0,2,1:T(8,128)(2,1)} %bitcast.21) | data formatting | bytes 33554432 | tf_op jit(solution)/shard_map/while | solution.py:35
  363.7 4.3 broadcast_in_dim.47
  368.0 118.7 %while.13 = (s32[]{:T(128)}, f32[128,128,128]{2,1,0:T(8,128)}, s32[128]{0:T(128)S(1)}, bf16[1024,64,128]{2,0,1:T(8,128)(2,1)}, s32[128]{0:T(128)S(1)}, /*index=5...) while((s32[]{:T(128)}, f32[128,128,128]{2,1,0:T(8,128)}, s32[128]{0:T(128)S(1)}, ...), condition=%wide.region_1.0_spmd, body=%wide.region_0.1_spmd.sunk | while | flops 1082657152 | bytes 54535460 | solution.py:35
  368.0 8.0 gather_fusion
  376.0 10.8 %gather_fusion.1 = bf16[32,1024,128]{2,1,0:T(8,128)(2,1)} fusion(bf16[1024,64,128]{2,0,1:T(8,128)(2,1)} %get-tuple-element.213, s32[1024]{0:T(1024)S(1)} %pad_clamp_fusion.5), kind=kCustom, calls=%fused_computation.clone.1 | custom fusion | bytes 16777344 | tf_op jit(solution)/shard_map/while/body/eval_jaxpr/jit(_take)/gather | solution.py:25
  386.8 10.8 %add_dynamic-update-slice_fusion.2 = f32[128,128,128]{2,1,0:T(8,128)} fusion(f32[128,128,128]{2,1,0:T(8,128)} %get-tuple-element.201, s32[]{:T(128)S(6)} %select_n.70, bf16[32,1024,128]{2,1,0:T(8,128)(2,1)} %gather_fusion, pred[32]{0:T(512)(128)(4,1)S(1)} %get-tuple-element.187, bf16[32,1024,128]{2,1,0:T(8,128)(2,1)} %gather_fusion.1, ...), kind=kOutput, calls=%fused_computation.10.clone.1 | convolution fusion | flops 1082654720 | bytes 20971588 | tf_op jit(solution)/shard_map/while/body/eval_jaxpr/rkc,rkd->kcd/dot_general | solution.py:27
  397.7 8.0 gather_fusion
  405.7 10.8 %gather_fusion.1 = bf16[32,1024,128]{2,1,0:T(8,128)(2,1)} fusion(bf16[1024,64,128]{2,0,1:T(8,128)(2,1)} %get-tuple-element.213, s32[1024]{0:T(1024)S(1)} %pad_clamp_fusion.5), kind=kCustom, calls=%fused_computation.clone.1 | custom fusion | bytes 16777344 | tf_op jit(solution)/shard_map/while/body/eval_jaxpr/jit(_take)/gather | solution.py:25
  416.4 10.9 %add_dynamic-update-slice_fusion.2 = f32[128,128,128]{2,1,0:T(8,128)} fusion(f32[128,128,128]{2,1,0:T(8,128)} %get-tuple-element.201, s32[]{:T(128)S(6)} %select_n.70, bf16[32,1024,128]{2,1,0:T(8,128)(2,1)} %gather_fusion, pred[32]{0:T(512)(128)(4,1)S(1)} %get-tuple-element.187, bf16[32,1024,128]{2,1,0:T(8,128)(2,1)} %gather_fusion.1, ...), kind=kOutput, calls=%fused_computation.10.clone.1 | convolution fusion | flops 1082654720 | bytes 20971588 | tf_op jit(solution)/shard_map/while/body/eval_jaxpr/rkc,rkd->kcd/dot_general | solution.py:27
  427.4 7.9 gather_fusion
  435.3 10.8 %gather_fusion.1 = bf16[32,1024,128]{2,1,0:T(8,128)(2,1)} fusion(bf16[1024,64,128]{2,0,1:T(8,128)(2,1)} %get-tuple-element.213, s32[1024]{0:T(1024)S(1)} %pad_clamp_fusion.5), kind=kCustom, calls=%fused_computation.clone.1 | custom fusion | bytes 16777344 | tf_op jit(solution)/shard_map/while/body/eval_jaxpr/jit(_take)/gather | solution.py:25
  446.1 10.8 %add_dynamic-update-slice_fusion.2 = f32[128,128,128]{2,1,0:T(8,128)} fusion(f32[128,128,128]{2,1,0:T(8,128)} %get-tuple-element.201, s32[]{:T(128)S(6)} %select_n.70, bf16[32,1024,128]{2,1,0:T(8,128)(2,1)} %gather_fusion, pred[32]{0:T(512)(128)(4,1)S(1)} %get-tuple-element.187, bf16[32,1024,128]{2,1,0:T(8,128)(2,1)} %gather_fusion.1, ...), kind=kOutput, calls=%fused_computation.10.clone.1 | convolution fusion | flops 1082654720 | bytes 20971588 | tf_op jit(solution)/shard_map/while/body/eval_jaxpr/rkc,rkd->kcd/dot_general | solution.py:27
  457.0 7.9 gather_fusion
  465.0 10.8 %gather_fusion.1 = bf16[32,1024,128]{2,1,0:T(8,128)(2,1)} fusion(bf16[1024,64,128]{2,0,1:T(8,128)(2,1)} %get-tuple-element.213, s32[1024]{0:T(1024)S(1)} %pad_clamp_fusion.5), kind=kCustom, calls=%fused_computation.clone.1 | custom fusion | bytes 16777344 | tf_op jit(solution)/shard_map/while/body/eval_jaxpr/jit(_take)/gather | solution.py:25
  475.8 10.8 %add_dynamic-update-slice_fusion.2 = f32[128,128,128]{2,1,0:T(8,128)} fusion(f32[128,128,128]{2,1,0:T(8,128)} %get-tuple-element.201, s32[]{:T(128)S(6)} %select_n.70, bf16[32,1024,128]{2,1,0:T(8,128)(2,1)} %gather_fusion, pred[32]{0:T(512)(128)(4,1)S(1)} %get-tuple-element.187, bf16[32,1024,128]{2,1,0:T(8,128)(2,1)} %gather_fusion.1, ...), kind=kOutput, calls=%fused_computation.10.clone.1 | convolution fusion | flops 1082654720 | bytes 20971588 | tf_op jit(solution)/shard_map/while/body/eval_jaxpr/rkc,rkd->kcd/dot_general | solution.py:27
  486.6 7.2 broadcast_multiply_fusion
  493.9 291.6 %all-reduce.2.cloned.1.call-done = f32[128,128,128]{2,1,0:T(8,128)} async-done(((f32[128,128,128]{2,1,0:T(8,128)}), f32[128,128,128]{2,1,0:T(8,128)}) %all-reduce.2.cloned.1.call-update) | async-done | bytes 8388624 | tf_op jit(solution)/shard_map/psum | solution.py:41
  785.5 6.1 multiply_reduce_fusion
  791.6 20.0 %psum.15 = f32[]{:T(128)} all-reduce(f32[]{:T(128)} %multiply_reduce_fusion), channel_id=1, replica_groups=mesh['dp'=32,'tensor'=8] {'tensor'}, use_global_device_ids=true, to_apply=%region_4.5 | all-reduce | flops 1 | bytes 8 | tf_op jit(solution)/shard_map/psum | solution.py:42
  812.3 1.7 bitcast_subtract_fusion
  (23 shorter events, 0.5 us)
Async XLA Ops:
  6.5 334.8 %all-gather.2.cloned.1.call-start = ((), (), s32[]{:S(2)}) async-start(), calls=%async_computation | async-start | bytes 18874368 | tf_op jit(solution)/shard_map/all_gather | solution.py:17
  10.6 774.8 %all-reduce.2.cloned.1.call-start = ((), (), s32[]{:S(2)}) async-start(), calls=%async_computation.1 | async-start | bytes 16777216 | tf_op jit(solution)/shard_map/psum | solution.py:41
  363.7 4.3 copy-start.1
  363.7 4.3 copy-start.2
  493.8 318.5 %copy-start = (f32[1,4,128,128]{3,2,1,0:T(8,128)S(1)}, f32[1,4,128,128]{3,2,1,0:T(8,128)}, u32[]{:S(2)}) copy-start(f32[1,4,128,128]{3,2,1,0:T(8,128)} %param.10) | copy-start | bytes 786436
Sparse Core Ops, SparseCore 0:
  10.8 330.4 all-gather.1
  494.0 291.4 all-reduce.1
where the time goes:
time: 822 us; the launch traced here: 821 us
  waiting for transfers between devices  602 us (73%)
  local copies, waits for them, and re-layouts  126 us (15%)
  matrix products  43.4 us (5%)
  blocking collectives  20 us (2%)
  other arithmetic  15.4 us (2%)
  between operations  14.8 us (2%)
    all_gather x1, waiting for transfers between devices, on_device(): shard_rows = lax.all_gather(tokens, 'tensor', axis=0, tiled=True)  310 us
    psum x1, waiting for transfers between devices, on_device(): summed = lax.psum(block_grads, 'dp')  292 us
    dot_general x4, matrix products, one_group(): jnp.einsum('rkc,rkd->kcd', token_cols, grad_cols, preferred_element_type=...  43.4 us
    gather x4, local copies, waits for them, and re-layouts, one_group(): token_cols = jnp.take(token_tiles, row_ids, axis=1)  43.1 us
    while x2, local copies, waits for them, and re-layouts, on_device(): block_grads = lax.fori_loop(0, group_trips, one_group, zero_grads)  32.4 us
    gather x4, local copies, waits for them, and re-layouts, one_group(): grad_cols = jnp.take(grad_tiles, col_ids, axis=1)  31.8 us
    psum x1, blocking collectives, on_device(): square_sum = lax.psum(jnp.sum(summed * summed), 'tensor')  20 us
  transfers between devices with their start and end apart: 2, of which 2 were waited for; matrix products, arithmetic and copies ran while one was open for 2% of the time, Pallas kernels for 0%

commit v1 on v0

--- a/solution.py
+++ b/solution.py
@@ -14,7 +14,9 @@
     col_blocks = out_grad.shape[1] // block_size
     group_trips = slot_count // GROUP
     zero_grads = jnp.zeros((slot_count, block_size, block_size), jnp.float32)
-    shard_rows = lax.all_gather(tokens, "tensor", axis=0, tiled=True)
+    shard_rows = jnp.concatenate(
+        lax.all_to_all(jnp.stack([tokens] * lax.axis_size("tensor")), "tensor", 0, 0), axis=0
+    )
     row_count = shard_rows.shape[0]
     token_tiles = shard_rows.reshape(row_count, row_blocks, block_size)
     grad_tiles = out_grad.reshape(row_count, col_blocks, block_size)

time: 822 us -> 708 us (0.86)
  waiting for transfers between devices: 602 us -> 456 us
  local copies, waits for them, and re-layouts: 126 us -> 151 us
    all_gather x1 -> x0, waiting for transfers between devices: 310 us -> none  [on_device(): shard_rows = lax.all_gather(tokens, 'tensor', axis=0, tiled=True)]
    all_to_all x0 -> x1, waiting for transfers between devices: none -> 164 us  [on_device(): lax.all_to_all(jnp.stack([tokens] * lax.axis_size('tensor')), 'tensor', 0...]
    while x2, local copies, waits for them, and re-layouts: 32.4 us -> 46 us  [on_device(): block_grads = lax.fori_loop(0, group_trips, one_group, zero_grads)]
  transfers between devices with their start and end apart: 2 -> 2, of which waited for: 2 -> 2; matrix products, arithmetic and copies ran while one was open for 2% -> 3% of each run, Pallas kernels for 0% -> 0%
where the time goes in v1:
time: 708 us; the launch traced here: 707 us
  waiting for transfers between devices  456 us (64%)
  local copies, waits for them, and re-layouts  151 us (21%)
  matrix products  43.4 us (6%)
  blocking collectives  20 us (3%)
  other arithmetic  15.4 us (2%)
  between operations  14.8 us (2%)
    psum x1, waiting for transfers between devices, on_device(): summed = lax.psum(block_grads, 'dp')  292 us
    all_to_all x1, waiting for transfers between devices, on_device(): lax.all_to_all(jnp.stack([tokens] * lax.axis_size('tensor')), 'tensor', 0...  164 us
    while x2, local copies, waits for them, and re-layouts, on_device(): block_grads = lax.fori_loop(0, group_trips, one_group, zero_grads)  46 us
    dot_general x4, matrix products, one_group(): jnp.einsum('rkc,rkd->kcd', token_cols, grad_cols, preferred_element_type=...  43.4 us
    gather x4, local copies, waits for them, and re-layouts, one_group(): token_cols = jnp.take(token_tiles, row_ids, axis=1)  43.1 us
    gather x4, local copies, waits for them, and re-layouts, one_group(): grad_cols = jnp.take(grad_tiles, col_ids, axis=1)  31.7 us
    psum x1, blocking collectives, on_device(): square_sum = lax.psum(jnp.sum(summed * summed), 'tensor')  20 us
    unnamed x8, local copies, waits for them, and re-layouts  19.7 us
  transfers between devices with their start and end apart: 2, of which 2 were waited for; matrix products, arithmetic and copies ran while one was open for 3% of the time, Pallas kernels for 0%

profile of v1, /device:TPU:4, one launch (start us, length us, event | category | flops | bytes accessed | tf_op | source)
XLA Modules:
  0.0 706.5 jit_solution(3680753333981385865)
XLA Ops:
  6.5 6.8 stack.2
  13.4 5.7 all-to-all-start
  19.2 10.0 %copy.13 = bf16[1024,3328]{0,1:T(8,128)(2,1)} copy(bf16[1024,3328]{1,0:T(8,128)(2,1)} %param.9) | data formatting | bytes 13631488 | tf_op args[1]
  29.1 9.9 %copy.15 = bf16[1024,26,128]{2,0,1:T(8,128)(2,1)} copy(bf16[1024,26,128]{0,2,1:T(8,128)(2,1)} %bitcast.23) | data formatting | bytes 13631488 | tf_op jit(solution)/shard_map/while | solution.py:37
  39.7 163.9 %all-to-all-done = bf16[8,128,8192]{2,1,0:T(8,128)(2,1)} async-done(((bf16[8,128,8192]{2,1,0:T(8,128)(2,1)}), bf16[8,128,8192]{2,1,0:T(8,128)(2,1)}, u32[]{:S(2)}, u32[]{:S(2)}) %all-to-all-start) | async-done | bytes 16777248 | tf_op jit(solution)/shard_map/all_to_all | solution.py:18
  203.7 9.7 %copy.17 = bf16[128,8,64,128]{3,2,1,0:T(8,128)(2,1)S(1)} copy(bf16[128,8,64,128]{3,1,2,0:T(8,128)(2,1)} %bitcast.6) | data formatting | bytes 33554432
  213.4 36.0 %copy.14 = bf16[1024,64,128]{2,0,1:T(8,128)(2,1)} copy(bf16[1024,64,128]{2,1,0:T(8,128)(2,1)S(1)} %bitcast.22) | data formatting | bytes 33554432 | tf_op jit(solution)/shard_map/while | solution.py:37
  253.7 118.6 %while.13 = (s32[]{:T(128)}, f32[128,128,128]{2,1,0:T(8,128)}, s32[128]{0:T(128)S(1)}, bf16[1024,64,128]{2,0,1:T(8,128)(2,1)}, s32[128]{0:T(128)S(1)}, /*index=5...) while((s32[]{:T(128)}, f32[128,128,128]{2,1,0:T(8,128)}, s32[128]{0:T(128)S(1)}, ...), condition=%wide.region_1.0_spmd, body=%wide.region_0.1_spmd.sunk | while | flops 1082657152 | bytes 54535460 | solution.py:37
  253.7 7.9 %gather_fusion = bf16[32,1024,128]{2,1,0:T(8,128)(2,1)} fusion(bf16[1024,26,128]{2,0,1:T(8,128)(2,1)} %get-tuple-element.215, s32[1024]{0:T(1024)S(1)} %pad_clamp_fusion.4), kind=kCustom, calls=%fused_computation.1.clone.1 | custom fusion | bytes 16777344 | tf_op jit(solution)/shard_map/while/body/eval_jaxpr/jit(_take)/gather | solution.py:28
  261.7 10.8 %gather_fusion.1 = bf16[32,1024,128]{2,1,0:T(8,128)(2,1)} fusion(bf16[1024,64,128]{2,0,1:T(8,128)(2,1)} %get-tuple-element.213, s32[1024]{0:T(1024)S(1)} %pad_clamp_fusion.5), kind=kCustom, calls=%fused_computation.clone.1 | custom fusion | bytes 16777344 | tf_op jit(solution)/shard_map/while/body/eval_jaxpr/jit(_take)/gather | solution.py:27
  272.5 10.8 %add_dynamic-update-slice_fusion.2 = f32[128,128,128]{2,1,0:T(8,128)} fusion(f32[128,128,128]{2,1,0:T(8,128)} %get-tuple-element.201, s32[]{:T(128)S(6)} %select_n.70, bf16[32,1024,128]{2,1,0:T(8,128)(2,1)} %gather_fusion, pred[32]{0:T(512)(128)(4,1)S(1)} %get-tuple-element.187, bf16[32,1024,128]{2,1,0:T(8,128)(2,1)} %gather_fusion.1, ...), kind=kOutput, calls=%fused_computation.10.clone.1 | convolution fusion | flops 1082654720 | bytes 20971588 | tf_op jit(solution)/shard_map/while/body/eval_jaxpr/rkc,rkd->kcd/dot_general | solution.py:29
  283.4 7.9 %gather_fusion = bf16[32,1024,128]{2,1,0:T(8,128)(2,1)} fusion(bf16[1024,26,128]{2,0,1:T(8,128)(2,1)} %get-tuple-element.215, s32[1024]{0:T(1024)S(1)} %pad_clamp_fusion.4), kind=kCustom, calls=%fused_computation.1.clone.1 | custom fusion | bytes 16777344 | tf_op jit(solution)/shard_map/while/body/eval_jaxpr/jit(_take)/gather | solution.py:28
  291.3 10.8 %gather_fusion.1 = bf16[32,1024,128]{2,1,0:T(8,128)(2,1)} fusion(bf16[1024,64,128]{2,0,1:T(8,128)(2,1)} %get-tuple-element.213, s32[1024]{0:T(1024)S(1)} %pad_clamp_fusion.5), kind=kCustom, calls=%fused_computation.clone.1 | custom fusion | bytes 16777344 | tf_op jit(solution)/shard_map/while/body/eval_jaxpr/jit(_take)/gather | solution.py:27
  302.1 10.9 %add_dynamic-update-slice_fusion.2 = f32[128,128,128]{2,1,0:T(8,128)} fusion(f32[128,128,128]{2,1,0:T(8,128)} %get-tuple-element.201, s32[]{:T(128)S(6)} %select_n.70, bf16[32,1024,128]{2,1,0:T(8,128)(2,1)} %gather_fusion, pred[32]{0:T(512)(128)(4,1)S(1)} %get-tuple-element.187, bf16[32,1024,128]{2,1,0:T(8,128)(2,1)} %gather_fusion.1, ...), kind=kOutput, calls=%fused_computation.10.clone.1 | convolution fusion | flops 1082654720 | bytes 20971588 | tf_op jit(solution)/shard_map/while/body/eval_jaxpr/rkc,rkd->kcd/dot_general | solution.py:29
  313.1 7.9 %gather_fusion = bf16[32,1024,128]{2,1,0:T(8,128)(2,1)} fusion(bf16[1024,26,128]{2,0,1:T(8,128)(2,1)} %get-tuple-element.215, s32[1024]{0:T(1024)S(1)} %pad_clamp_fusion.4), kind=kCustom, calls=%fused_computation.1.clone.1 | custom fusion | bytes 16777344 | tf_op jit(solution)/shard_map/while/body/eval_jaxpr/jit(_take)/gather | solution.py:28
  321.0 10.8 %gather_fusion.1 = bf16[32,1024,128]{2,1,0:T(8,128)(2,1)} fusion(bf16[1024,64,128]{2,0,1:T(8,128)(2,1)} %get-tuple-element.213, s32[1024]{0:T(1024)S(1)} %pad_clamp_fusion.5), kind=kCustom, calls=%fused_computation.clone.1 | custom fusion | bytes 16777344 | tf_op jit(solution)/shard_map/while/body/eval_jaxpr/jit(_take)/gather | solution.py:27
  331.8 10.8 %add_dynamic-update-slice_fusion.2 = f32[128,128,128]{2,1,0:T(8,128)} fusion(f32[128,128,128]{2,1,0:T(8,128)} %get-tuple-element.201, s32[]{:T(128)S(6)} %select_n.70, bf16[32,1024,128]{2,1,0:T(8,128)(2,1)} %gather_fusion, pred[32]{0:T(512)(128)(4,1)S(1)} %get-tuple-element.187, bf16[32,1024,128]{2,1,0:T(8,128)(2,1)} %gather_fusion.1, ...), kind=kOutput, calls=%fused_computation.10.clone.1 | convolution fusion | flops 1082654720 | bytes 20971588 | tf_op jit(solution)/shard_map/while/body/eval_jaxpr/rkc,rkd->kcd/dot_general | solution.py:29
  342.7 7.9 %gather_fusion = bf16[32,1024,128]{2,1,0:T(8,128)(2,1)} fusion(bf16[1024,26,128]{2,0,1:T(8,128)(2,1)} %get-tuple-element.215, s32[1024]{0:T(1024)S(1)} %pad_clamp_fusion.4), kind=kCustom, calls=%fused_computation.1.clone.1 | custom fusion | bytes 16777344 | tf_op jit(solution)/shard_map/while/body/eval_jaxpr/jit(_take)/gather | solution.py:28
  350.6 10.8 %gather_fusion.1 = bf16[32,1024,128]{2,1,0:T(8,128)(2,1)} fusion(bf16[1024,64,128]{2,0,1:T(8,128)(2,1)} %get-tuple-element.213, s32[1024]{0:T(1024)S(1)} %pad_clamp_fusion.5), kind=kCustom, calls=%fused_computation.clone.1 | custom fusion | bytes 16777344 | tf_op jit(solution)/shard_map/while/body/eval_jaxpr/jit(_take)/gather | solution.py:27
  361.4 10.8 %add_dynamic-update-slice_fusion.2 = f32[128,128,128]{2,1,0:T(8,128)} fusion(f32[128,128,128]{2,1,0:T(8,128)} %get-tuple-element.201, s32[]{:T(128)S(6)} %select_n.70, bf16[32,1024,128]{2,1,0:T(8,128)(2,1)} %gather_fusion, pred[32]{0:T(512)(128)(4,1)S(1)} %get-tuple-element.187, bf16[32,1024,128]{2,1,0:T(8,128)(2,1)} %gather_fusion.1, ...), kind=kOutput, calls=%fused_computation.10.clone.1 | convolution fusion | flops 1082654720 | bytes 20971588 | tf_op jit(solution)/shard_map/while/body/eval_jaxpr/rkc,rkd->kcd/dot_general | solution.py:29
  372.2 7.2 %broadcast_multiply_fusion = f32[128,128,128]{2,1,0:T(8,128)} fusion(f32[128,128,128]{2,1,0:T(8,128)} %get-tuple-element.114, f32[128]{0:T(128)S(1)} %compare_convert_fusion), kind=kLoop, calls=%fused_computation.19 | loop fusion | flops 2097152 | bytes 16777728 | tf_op jit(solution)/shard_map/mul | solution.py:39
  379.4 291.7 %all-reduce.2.cloned.1.call-done = f32[128,128,128]{2,1,0:T(8,128)} async-done(((f32[128,128,128]{2,1,0:T(8,128)}), f32[128,128,128]{2,1,0:T(8,128)}) %all-reduce.2.cloned.1.call-update) | async-done | bytes 8388624 | tf_op jit(solution)/shard_map/psum | solution.py:43
  671.1 6.1 multiply_reduce_fusion
  677.3 20.0 %psum.15 = f32[]{:T(128)} all-reduce(f32[]{:T(128)} %multiply_reduce_fusion), channel_id=1, replica_groups=mesh['dp'=32,'tensor'=8] {'tensor'}, use_global_device_ids=true, to_apply=%region_4.5 | all-reduce | flops 1 | bytes 8 | tf_op jit(solution)/shard_map/psum | solution.py:44
  (23 shorter events, 6.4 us)
Async XLA Ops:
  13.4 190.3 %all-to-all-start = ((bf16[8,128,8192]{2,1,0:T(8,128)(2,1)}), bf16[8,128,8192]{2,1,0:T(8,128)(2,1)}, u32[]{:S(2)}, u32[]{:S(2)}) async-start(bf16[8,128,8192]{2,1,0:T(8,128)(2,1)} %stack.2), calls=%async_computation | async-start | bytes 33554432 | tf_op jit(solution)/shard_map/all_to_all | solution.py:18
  19.1 652.0 %all-reduce.2.cloned.1.call-start = ((), (), s32[]{:S(2)}) async-start(), calls=%async_computation.1 | async-start | bytes 16777216 | tf_op jit(solution)/shard_map/psum | solution.py:43
  249.4 4.3 copy-start.1
  249.4 4.3 copy-start.2
  379.4 318.6 %copy-start = (f32[1,4,128,128]{3,2,1,0:T(8,128)S(1)}, f32[1,4,128,128]{3,2,1,0:T(8,128)}, u32[]{:S(2)}) copy-start(f32[1,4,128,128]{3,2,1,0:T(8,128)} %param.10) | copy-start | bytes 786436
Sparse Core Ops, SparseCore 0:
  379.6 291.5 all-reduce.1
